TPU v7x, 32 devices: a whole 2x2x4 slice. The times are simulated.
32 devices in a mesh: dp: 8 (over z, x), seq: 4 (over y, core).
Axes of the slice: x: 2, y: 2, z: 4, core: 2. Of those that a mesh axis runs over, the one named last changes fastest.
Arguments:
- hidden_in: bfloat16 [16384, 512], P(('dp', 'seq')), may hold values from -6 to 6
- memory: bfloat16 [8192, 512], P(('dp', 'seq')), may hold values from -6 to 6
- lengths: int32 [8], P('dp'), may hold values from 512 to 2048, as said below
- memory_lengths: int32 [8], P('dp'), may hold values from 256 to 1024, as said below
- self_in: bfloat16 [512, 1536], P('dp'), may hold values from -0.25 to 0.25
- self_out: bfloat16 [512, 512], P('dp'), may hold values from -1.5 to 1.5
- cross_query: bfloat16 [512, 512], P('dp'), may hold values from -0.25 to 0.25
- cross_memory: bfloat16 [512, 1024], P('dp'), may hold values from -0.25 to 0.25
- cross_out: bfloat16 [512, 512], P('dp'), may hold values from -1 to 1
- ffn_in: bfloat16 [512, 2048], P('dp'), may hold values from -0.25 to 0.25
- ffn_bias: bfloat16 [2048], P('dp'), may hold values from -3 to 3
- ffn_out: bfloat16 [2048, 512], P('dp'), may hold values from -0.125 to 0.125
- out_bias: bfloat16 [512], P('dp'), may hold values from -2 to 2
- gain_self: bfloat16 [512], P('dp'), may hold values from 0.099609375 to 1.8984375
- shift_self: bfloat16 [512], P('dp'), may hold values from -2 to 2
- gain_cross: bfloat16 [512], P('dp'), may hold values from 0.099609375 to 1.8984375
- shift_cross: bfloat16 [512], P('dp'), may hold values from -2 to 2
- gain_ffn: bfloat16 [512], P('dp'), may hold values from 0.099609375 to 1.8984375
- shift_ffn: bfloat16 [512], P('dp'), may hold values from -2 to 2
- exit_weight: bfloat16 [512], P('dp'), may hold values from -0.25 to 0.25
- grad_result: bfloat16 [16384, 512], P(('dp', 'seq')), may hold values from -6 to 6
- grad_halting: float32 [16384], P(('dp', 'seq')), may hold values from -6 to 6
Outputs:
- result: bfloat16 [16384, 512], P(('dp', 'seq'))
- halting: float32 [16384], P(('dp', 'seq'))
- grad_hidden: float32 [16384, 512], P(('dp', 'seq'))
- grad_memory: float32 [8192, 512], P(('dp', 'seq'))
- grad_self_in: float32 [512, 1536], P('dp')
- grad_self_out: float32 [512, 512], P('dp')
- grad_cross_query: float32 [512, 512], P('dp')
- grad_cross_memory: float32 [512, 1024], P('dp')
- grad_cross_out: float32 [512, 512], P('dp')
- grad_ffn_in: float32 [512, 2048], P('dp')
- grad_ffn_bias: float32 [2048], P('dp')
- grad_ffn_out: float32 [2048, 512], P('dp')
- grad_out_bias: float32 [512], P('dp')
- grad_gain_self: float32 [512], P('dp')
- grad_shift_self: float32 [512], P('dp')
- grad_gain_cross: float32 [512], P('dp')
- grad_shift_cross: float32 [512], P('dp')
- grad_gain_ffn: float32 [512], P('dp')
- grad_shift_ffn: float32 [512], P('dp')
- grad_exit_weight: float32 [512], P('dp')
Inputs may be any that keep to these rules, and one draw needn't show every extreme that they name: Positions from lengths[s] to 2047 of sequence s are padding; some sequence has exactly 2048 valid positions in every draw. Memory positions from memory_lengths[s] on are padding; some sequence has exactly 1024 in every draw.
All inputs are finite; a program needn't handle non-finite values.
Results may differ from a plain program's by a relative error of at most 0.02.
The roundings to bfloat16 on the way count: a program that leaves them out, or rounds other values in their place, can miss the bound.
Values may be sent and summed in bfloat16 or wider, within the bound.
A program may use at most 128 MiB of HBM per device.

v0:
```python
import jax
import jax.numpy as jnp
from jax import lax
from jax.sharding import PartitionSpec as P

HD = 64


epsilon = 1e-05
masked_score = -1e30
gelu_scale = 0.7978845608028654
gelu_cubic = 0.044715


def matmul(left, right):
    return jnp.dot(left, right, preferred_element_type=jnp.float32)


def left_contract(left, right):
    return lax.dot_general(
        left, right, (((0,), (0,)), ((), ())), preferred_element_type=jnp.float32
    )


def back_product(left, right):
    return lax.dot_general(
        left, right, (((1,), (1,)), ((), ())), preferred_element_type=jnp.float32
    )


def smooth_gate(value):
    return 0.5 * value * (1.0 + jnp.tanh(gelu_scale * (value + gelu_cubic * value * value * value)))


def smooth_slope(value):
    bent = jnp.tanh(gelu_scale * (value + gelu_cubic * value * value * value))
    return 0.5 * (1.0 + bent) + 0.5 * value * (1.0 - bent * bent) * gelu_scale * (
        1.0 + 3.0 * gelu_cubic * value * value
    )


def norm_forward(value, gain, shift):
    average = jnp.mean(value, axis=-1, keepdims=True)
    centred = value - average
    variance = jnp.mean(centred * centred, axis=-1, keepdims=True)
    inverse = lax.rsqrt(variance + epsilon)
    unit_rows = centred * inverse
    return (unit_rows * gain + shift, unit_rows, inverse)


def norm_backward(grad_out, unit_rows, inverse, gain):
    scaled = grad_out * gain
    first_mean = jnp.mean(scaled, axis=-1, keepdims=True)
    second_mean = jnp.mean(scaled * unit_rows, axis=-1, keepdims=True)
    grad_in = inverse * (scaled - first_mean - unit_rows * second_mean)
    return (grad_in, jnp.sum(grad_out * unit_rows, axis=0), jnp.sum(grad_out, axis=0))


def key_mask(first_row, block_rows, key_rows, key_limit, causal):
    key_place = jnp.arange(key_rows)
    allowed = key_place[None, :] < key_limit
    if causal:
        allowed = allowed & (key_place[None, :] <= first_row + jnp.arange(block_rows)[:, None])
    return allowed


def attend_forward(queries, keys_in, values_in, key_limit, causal):
    query_rows, model_width = queries.shape
    head_count = model_width // HD
    block_rows = min(512, query_rows)
    blocks = query_rows // block_rows
    key_rows = keys_in.shape[0]
    key_heads = keys_in.reshape(key_rows, head_count, HD)
    value_heads = values_in.reshape(key_rows, head_count, HD)
    score_scale = HD ** (-0.5)

    def one_block(block_index):
        first_row = block_index * block_rows
        query_block = lax.dynamic_slice_in_dim(queries, first_row, block_rows, 0).reshape(
            block_rows, head_count, HD
        )
        scores = (
            jnp.einsum("qhd,khd->hqk", query_block, key_heads, preferred_element_type=jnp.float32)
            * score_scale
        )
        allowed = key_mask(first_row, block_rows, key_rows, key_limit, causal)
        scores = jnp.where(allowed[None], scores, masked_score)
        largest = jnp.max(scores, axis=-1, keepdims=True)
        powers = jnp.exp(scores - largest)
        totals = jnp.sum(powers, axis=-1, keepdims=True)
        attention = (powers / totals).astype(jnp.bfloat16)
        attended = jnp.einsum(
            "hqk,khd->qhd", attention, value_heads, preferred_element_type=jnp.float32
        )
        return (
            attended.reshape(block_rows, model_width).astype(jnp.bfloat16),
            largest[..., 0] + jnp.log(totals[..., 0]),
        )

    attended, spread = lax.map(one_block, jnp.arange(blocks))
    return (attended.reshape(query_rows, model_width), spread)


def attend_backward(queries, keys_in, values_in, spread, grad_mixed, key_limit, causal):
    query_rows, model_width = queries.shape
    head_count = model_width // HD
    block_rows = min(512, query_rows)
    blocks = query_rows // block_rows
    key_rows = keys_in.shape[0]
    key_heads = keys_in.reshape(key_rows, head_count, HD)
    value_heads = values_in.reshape(key_rows, head_count, HD)
    score_scale = HD ** (-0.5)

    def one_block(running, block_items):
        grad_keys, grad_values = running
        block_index, block_spread = block_items
        first_row = block_index * block_rows
        query_block = lax.dynamic_slice_in_dim(queries, first_row, block_rows, 0).reshape(
            block_rows, head_count, HD
        )
        grad_block = lax.dynamic_slice_in_dim(grad_mixed, first_row, block_rows, 0).reshape(
            block_rows, head_count, HD
        )
        scores = (
            jnp.einsum("qhd,khd->hqk", query_block, key_heads, preferred_element_type=jnp.float32)
            * score_scale
        )
        allowed = key_mask(first_row, block_rows, key_rows, key_limit, causal)
        scores = jnp.where(allowed[None], scores, masked_score)
        recalled = jnp.exp(scores - block_spread[:, :, None])
        grad_probs = jnp.einsum(
            "qhd,khd->hqk", grad_block, value_heads, preferred_element_type=jnp.float32
        )
        weighted = jnp.sum(recalled * grad_probs, axis=-1, keepdims=True)
        grad_scores = (recalled * (grad_probs - weighted)).astype(jnp.bfloat16)
        grad_query = (
            jnp.einsum("hqk,khd->qhd", grad_scores, key_heads, preferred_element_type=jnp.float32)
            * score_scale
        )
        grad_keys = (
            grad_keys
            + jnp.einsum(
                "hqk,qhd->khd", grad_scores, query_block, preferred_element_type=jnp.float32
            )
            * score_scale
        )
        grad_values = grad_values + jnp.einsum(
            "hqk,qhd->khd",
            recalled.astype(jnp.bfloat16),
            grad_block,
            preferred_element_type=jnp.float32,
        )
        return (
            (grad_keys, grad_values),
            grad_query.reshape(block_rows, model_width).astype(jnp.bfloat16),
        )

    zero_state = jnp.zeros((key_rows, head_count, HD), jnp.float32)
    (grad_keys, grad_values), grad_queries = lax.scan(
        one_block, (zero_state, zero_state), (jnp.arange(blocks), spread)
    )
    return (
        grad_queries.reshape(query_rows, model_width),
        grad_keys.reshape(key_rows, model_width).astype(jnp.bfloat16),
        grad_values.reshape(key_rows, model_width).astype(jnp.bfloat16),
    )


def shards(
    hidden_in,
    memory,
    lengths,
    memory_lengths,
    self_in,
    self_out,
    cross_query,
    cross_memory,
    cross_out,
    ffn_in,
    ffn_bias,
    ffn_out,
    out_bias,
    gain_self,
    shift_self,
    gain_cross,
    shift_cross,
    gain_ffn,
    shift_ffn,
    exit_weight,
    grad_result,
    grad_halting,
):
    gathered = (
        lax.all_gather(self_in, "dp", axis=0, tiled=True),
        lax.all_gather(self_out, "dp", axis=0, tiled=True),
        lax.all_gather(cross_query, "dp", axis=0, tiled=True),
        lax.all_gather(cross_memory, "dp", axis=0, tiled=True),
        lax.all_gather(cross_out, "dp", axis=0, tiled=True),
        lax.all_gather(ffn_in, "dp", axis=0, tiled=True),
        lax.all_gather(ffn_bias, "dp", axis=0, tiled=True),
        lax.all_gather(ffn_out, "dp", axis=0, tiled=True),
        lax.all_gather(out_bias, "dp", axis=0, tiled=True),
        lax.all_gather(gain_self, "dp", axis=0, tiled=True),
        lax.all_gather(shift_self, "dp", axis=0, tiled=True),
        lax.all_gather(gain_cross, "dp", axis=0, tiled=True),
        lax.all_gather(shift_cross, "dp", axis=0, tiled=True),
        lax.all_gather(gain_ffn, "dp", axis=0, tiled=True),
        lax.all_gather(shift_ffn, "dp", axis=0, tiled=True),
        lax.all_gather(exit_weight, "dp", axis=0, tiled=True),
    )
    (
        joint_proj,
        mixer_proj,
        cross_proj,
        memory_proj,
        cross_back,
        inner_proj,
        inner_bias,
        outer_proj,
        outer_bias,
        gain_one,
        shift_one,
        gain_two,
        shift_two,
        gain_three,
        shift_three,
        exit_proj,
    ) = gathered
    gain_one = gain_one.astype(jnp.float32)
    gain_two = gain_two.astype(jnp.float32)
    gain_three = gain_three.astype(jnp.float32)
    token_rows, model_width = hidden_in.shape
    memory_rows = memory.shape[0]
    positions = lax.axis_index("seq") * token_rows + jnp.arange(token_rows)
    live_rows = (positions < lengths[0]).astype(jnp.float32)
    seq_limit = lengths[0]
    memory_limit = memory_lengths[0]
    hidden = hidden_in.astype(jnp.float32)
    normed_one, unit_one, inverse_one = norm_forward(
        hidden, gain_one, shift_one.astype(jnp.float32)
    )
    normed_one = normed_one.astype(jnp.bfloat16)
    packed = matmul(normed_one, joint_proj).astype(jnp.bfloat16).reshape(token_rows, 3, model_width)
    memory_pair = (
        matmul(memory, memory_proj).astype(jnp.bfloat16).reshape(memory_rows, 2, model_width)
    )
    packed_heads, memory_heads = (
        lax.all_to_all(packed, "seq", split_axis=2, concat_axis=0, tiled=True),
        lax.all_to_all(memory_pair, "seq", split_axis=2, concat_axis=0, tiled=True),
    )
    self_queries = packed_heads[:, 0]
    self_keys = packed_heads[:, 1]
    self_values = packed_heads[:, 2]
    memory_keys = memory_heads[:, 0]
    memory_values = memory_heads[:, 1]
    attended, spread_self = attend_forward(self_queries, self_keys, self_values, seq_limit, True)
    attended_tokens = lax.all_to_all(attended, "seq", split_axis=0, concat_axis=1, tiled=True)
    after_self = hidden + matmul(attended_tokens, mixer_proj)
    normed_two, unit_two, inverse_two = norm_forward(
        after_self, gain_two, shift_two.astype(jnp.float32)
    )
    normed_two = normed_two.astype(jnp.bfloat16)
    cross_queries = matmul(normed_two, cross_proj).astype(jnp.bfloat16)
    cross_heads = lax.all_to_all(cross_queries, "seq", split_axis=1, concat_axis=0, tiled=True)
    cross_mixed, spread_cross = attend_forward(
        cross_heads, memory_keys, memory_values, memory_limit, False
    )
    cross_tokens = lax.all_to_all(cross_mixed, "seq", split_axis=0, concat_axis=1, tiled=True)
    after_cross = after_self + matmul(cross_tokens, cross_back)
    normed_three, unit_three, inverse_three = norm_forward(
        after_cross, gain_three, shift_three.astype(jnp.float32)
    )
    normed_three = normed_three.astype(jnp.bfloat16)
    inner_pre = matmul(normed_three, inner_proj) + inner_bias.astype(jnp.float32)
    active = smooth_gate(inner_pre).astype(jnp.bfloat16)
    output = after_cross + matmul(active, outer_proj) + outer_bias.astype(jnp.float32)
    exit_column = exit_proj.astype(jnp.float32)
    halting = jax.nn.sigmoid(jnp.dot(output, exit_column, precision=lax.Precision.HIGHEST))
    grad_logit = grad_halting * live_rows * halting * (1.0 - halting)
    grad_exit = jnp.dot(grad_logit, output, precision=lax.Precision.HIGHEST)
    grad_output = (
        grad_result.astype(jnp.float32) * live_rows[:, None]
        + grad_logit[:, None] * exit_column[None, :]
    )
    grad_branch = grad_output.astype(jnp.bfloat16)
    grad_outer_bias = jnp.sum(grad_branch.astype(jnp.float32), axis=0)
    grad_outer = left_contract(active, grad_branch)
    grad_active = back_product(grad_branch, outer_proj)
    grad_inner = (grad_active * smooth_slope(inner_pre)).astype(jnp.bfloat16)
    grad_inner_bias = jnp.sum(grad_inner.astype(jnp.float32), axis=0)
    grad_inner_proj = left_contract(normed_three, grad_inner)
    grad_norm_three, grad_gain_three, grad_shift_three = norm_backward(
        back_product(grad_inner, inner_proj), unit_three, inverse_three, gain_three
    )
    grad_cross_res = grad_output + grad_norm_three
    grad_cross_branch = grad_cross_res.astype(jnp.bfloat16)
    grad_cross_back = left_contract(cross_tokens, grad_cross_branch)
    grad_cross_tokens = back_product(grad_cross_branch, cross_back).astype(jnp.bfloat16)
    grad_cross_mixed = lax.all_to_all(
        grad_cross_tokens, "seq", split_axis=1, concat_axis=0, tiled=True
    )
    grad_cross_q, grad_memory_k, grad_memory_v = attend_backward(
        cross_heads, memory_keys, memory_values, spread_cross, grad_cross_mixed, memory_limit, False
    )
    grad_query_home, grad_memory_home = (
        lax.all_to_all(grad_cross_q[:, None, :], "seq", split_axis=0, concat_axis=2, tiled=True),
        lax.all_to_all(
            jnp.stack([grad_memory_k, grad_memory_v], axis=1),
            "seq",
            split_axis=0,
            concat_axis=2,
            tiled=True,
        ),
    )
    grad_cross_queries = grad_query_home.reshape(token_rows, model_width)
    grad_memory_pair = grad_memory_home.reshape(memory_rows, 2 * model_width)
    grad_cross_proj = left_contract(normed_two, grad_cross_queries)
    grad_memory_proj = left_contract(memory, grad_memory_pair)
    grad_memory = back_product(grad_memory_pair, memory_proj)
    grad_norm_two, grad_gain_two, grad_shift_two = norm_backward(
        back_product(grad_cross_queries, cross_proj), unit_two, inverse_two, gain_two
    )
    grad_self_res = grad_cross_res + grad_norm_two
    grad_self_branch = grad_self_res.astype(jnp.bfloat16)
    grad_mixer = left_contract(attended_tokens, grad_self_branch)
    grad_attended = back_product(grad_self_branch, mixer_proj).astype(jnp.bfloat16)
    grad_attended_heads = lax.all_to_all(
        grad_attended, "seq", split_axis=1, concat_axis=0, tiled=True
    )
    grad_self_q, grad_self_k, grad_self_v = attend_backward(
        self_queries, self_keys, self_values, spread_self, grad_attended_heads, seq_limit, True
    )
    grad_packed = lax.all_to_all(
        jnp.stack([grad_self_q, grad_self_k, grad_self_v], axis=1),
        "seq",
        split_axis=0,
        concat_axis=2,
        tiled=True,
    ).reshape(token_rows, 3 * model_width)
    grad_joint = left_contract(normed_one, grad_packed)
    grad_norm_one, grad_gain_one, grad_shift_one = norm_backward(
        back_product(grad_packed, joint_proj), unit_one, inverse_one, gain_one
    )
    grad_hidden = grad_self_res + grad_norm_one
    grads = (
        grad_joint,
        grad_mixer,
        grad_cross_proj,
        grad_memory_proj,
        grad_cross_back,
        grad_inner_proj,
        grad_inner_bias,
        grad_outer,
        grad_outer_bias,
        grad_gain_one,
        grad_shift_one,
        grad_gain_two,
        grad_shift_two,
        grad_gain_three,
        grad_shift_three,
        grad_exit,
    )
    dp_count = lax.axis_size("dp")
    seq_count = lax.axis_size("seq")
    flat_grads = jnp.concatenate(
        [grad_part.reshape(dp_count, seq_count, -1) for grad_part in grads], axis=2
    )
    owned_rows = lax.psum_scatter(flat_grads, "dp", scatter_dimension=0, tiled=True)
    summed = lax.psum(owned_rows, "seq")
    pieces = []
    offset = 0
    for grad_part in grads:
        segment = grad_part.size // (dp_count * seq_count)
        shard_shape = (grad_part.shape[0] // dp_count,) + grad_part.shape[1:]
        pieces.append(summed[0, :, offset : offset + segment].reshape(shard_shape))
        offset = offset + segment
    return (output.astype(jnp.bfloat16), halting, grad_hidden, grad_memory) + tuple(pieces)


def solution(mesh):
    return jax.shard_map(
        shards,
        mesh=mesh,
        in_specs=(
            P(("dp", "seq"), None),
            P(("dp", "seq"), None),
            P("dp"),
            P("dp"),
            P("dp", None),
            P("dp", None),
            P("dp", None),
            P("dp", None),
            P("dp", None),
            P("dp", None),
            P("dp"),
            P("dp", None),
            P("dp"),
            P("dp"),
            P("dp"),
            P("dp"),
            P("dp"),
            P("dp"),
            P("dp"),
            P("dp"),
            P(("dp", "seq"), None),
            P(("dp", "seq")),
        ),
        out_specs=(
            P(("dp", "seq"), None),
            P(("dp", "seq")),
            P(("dp", "seq"), None),
            P(("dp", "seq"), None),
            P("dp", None),
            P("dp", None),
            P("dp", None),
            P("dp", None),
            P("dp", None),
            P("dp", None),
            P("dp"),
            P("dp", None),
            P("dp"),
            P("dp"),
            P("dp"),
            P("dp"),
            P("dp"),
            P("dp"),
            P("dp"),
            P("dp"),
        ),
        check_vma=False,
    )
```

profile of v0, /device:TPU:0, one launch (start us, length us, event | category | flops | bytes accessed | tf_op | source)
XLA Modules:
  0.0 1298.9 jit_solution(690356544465425151)
XLA Ops:
  18.8 23.5 %all-reduce.9 = (bf16[512]{0:T(512)(128)(2,1)S(1)}, bf16[512]{0:T(512)(128)(2,1)S(1)}, bf16[512]{0:T(512)(128)(2,1)S(1)}, bf16[512]{0:T(512)(128)(2,1)S(1)}, bf1...) all-reduce(bf16[512]{0:T(512)(128)(2,1)S(1)} %dynamic-update-slice., ...), channel_id=1, replica_groups=mesh['dp'=8,'seq'=4] {'dp'}, use_global_device_ids=true, to_apply=%add.1 | all-reduce | flops 4096 | bytes 16384
  42.6 14.5 %all-gather.6.cloned.1.call-done = bf16[512,1536]{1,0:T(8,128)(2,1)} async-done(((bf16[64,1536]{1,0:T(8,128)(2,1)}), bf16[512,1536]{1,0:T(8,128)(2,1)}) %all-gather.6.cloned.1.call-update) | async-done | bytes 1572880 | tf_op jit(solution)/shard_map/all_gather | solution.py:194
  57.2 3.7 convolution_convert_fusion
  65.3 3.6 all-to-all-start
  69.7 34.4 %all_gather.51 = bf16[512,512]{1,0:T(8,128)(2,1)} all-gather(bf16[64,512]{1,0:T(8,128)(2,1)S(1)} %copy-done.52), channel_id=1, replica_groups=mesh['dp'=8,'seq'=4] {'dp'}, dimensions={0}, use_global_device_ids=true | all-gather | bytes 589824 | tf_op jit(solution)/shard_map/all_gather | solution.py:195
  111.1 43.3 %while.54 = (s32[]{:T(128)}, bf16[4,512,128]{1,2,0:T(8,128)(2,1)S(1)}, f32[4,2,512]{2,1,0:T(2,128)S(1)}, s32[]{:T(128)}, s32[4]{0:T(128)S(1)}, /*index=5*/bf16[2...) while((s32[]{:T(128)}, ...), condition=%wide.region_5.6_spmd, body=%wide.region_2.5_spmd.sunk | while | flops 564200960 | bytes 31236300 | solution.py:100
  155.1 3.5 all-to-all-start.1
  158.6 33.4 %all_gather.54 = bf16[512,512]{1,0:T(8,128)(2,1)} all-gather(bf16[64,512]{1,0:T(8,128)(2,1)S(1)} %copy-done.53), channel_id=1, replica_groups=mesh['dp'=8,'seq'=4] {'dp'}, dimensions={0}, use_global_device_ids=true | all-gather | bytes 589824 | tf_op jit(solution)/shard_map/all_gather | solution.py:196
  196.1 4.1 all-to-all-start.3
  204.7 4.4 all-to-all-done.3
  209.1 3.5 all-to-all-start.2
  216.3 5.1 all-to-all-done.2
  223.7 37.3 %while.55 = (s32[]{:T(128)}, bf16[4,512,128]{1,2,0:T(8,128)(2,1)}, f32[4,2,512]{2,1,0:T(2,128)}, s32[]{:T(128)}, s32[4]{0:T(128)S(1)}, /*index=5*/bf16[2048,128]...) while((s32[]{:T(128)}, bf16[4,512,128]{1,2,0:T(8,128)(2,1)}, ...), condition=%wide.region_11.12_spmd, body=%wide.region_8.11_spmd.sunk | while | flops 281083904 | bytes 13930695 | solution.py:100
  261.0 3.5 all-to-all-start.4
  265.2 18.3 %all-gather = bf16[8,1,256]{2,1,0:T(2,128)(2,1)S(1)} all-gather(bf16[1,1,256]{2,1,0:T(2,128)(2,1)S(1)} %reshape.510), channel_id=1, replica_groups=mesh['dp'=8,'seq'=4] {'dp'}, dimensions={0}, use_global_device_ids=true | all-gather | bytes 4608 | tf_op jit(solution)/shard_map/all_gather | solution.py:200
  284.6 31.5 %all_gather.56 = bf16[512,512]{1,0:T(8,128)(2,1)S(1)} all-gather(bf16[64,512]{1,0:T(8,128)(2,1)S(1)} %copy-done.54), channel_id=1, replica_groups=mesh['dp'=8,'seq'=4] {'dp'}, dimensions={0}, use_global_device_ids=true | all-gather | bytes 589824 | tf_op jit(solution)/shard_map/all_gather | solution.py:198
  316.8 5.1 fusion.81
  322.0 5.8 fusion.91
  328.9 4.7 convert_reduce_fusion
  342.2 3.6 all-to-all-start.5
  345.9 8.8 all-to-all-done.5
  356.9 73.6 %while.56 = (s32[]{:T(128)}, f32[1024,2,64]{0,2,1:T(8,128)}, f32[1024,2,64]{0,2,1:T(8,128)}, bf16[4,512,128]{2,1,0:T(8,128)(2,1)}, s32[4]{0:T(128)}, /*index=5*/...) while((s32[]{:T(128)}, f32[1024,2,64]{0,2,1:T(8,128)}, ...), condition=%wide.region_18.19_spmd.clone, body=%wide.region_16.18_spmd.clone.sunk | while | flops 687603712 | bytes 53383484 | solution.py:159
  367.9 4.0 fusion.223
  386.4 4.2 fusion.223
  405.1 4.2 fusion.223
  423.8 4.2 fusion.223
  434.0 4.1 all-to-all-start.6
  438.2 6.7 fusion.77
  451.4 3.3 fusion.93
  462.5 4.1 all-to-all-start.7
  466.7 4.9 fusion.80
  475.5 4.6 all-to-all-start.9
  482.8 96.8 %while.57 = (s32[]{:T(128)}, f32[2048,2,64]{0,2,1:T(8,128)S(1)}, f32[2048,2,64]{0,2,1:T(8,128)}, bf16[4,512,128]{2,1,0:T(8,128)(2,1)}, s32[4]{0:T(128)S(1)}, /*i...) while((s32[]{:T(128)}, f32[2048,2,64]{0,2,1:T(8,128)S(1)}, ...), condition=%wide.region_23.24_spmd.clone, body=%wide.region_21.23_spmd.clone.sunk | while | flops 1377175040 | bytes 159551888 | solution.py:159
  488.6 3.0 multiply_reduce_fusion.14
  491.6 3.9 multiply_convert_fusion.8
  495.5 3.3 fusion.237
  500.2 3.6 fusion.238
  511.7 3.0 multiply_reduce_fusion.14
  514.8 3.9 multiply_convert_fusion.8
  518.7 3.3 fusion.237
  523.3 5.0 fusion.238
  536.3 3.0 multiply_reduce_fusion.14
  539.3 3.9 multiply_convert_fusion.8
  543.2 3.3 fusion.237
  547.9 5.0 fusion.238
  560.8 3.0 multiply_reduce_fusion.14
  563.9 3.9 multiply_convert_fusion.8
  567.8 3.3 fusion.237
  572.4 5.0 fusion.238
  581.8 10.7 copy.285
  592.5 4.5 all-to-all-start.8
  599.2 6.2 reshape.475
  605.6 6.1 reshape.477
  619.9 3.0 reshape.471
  624.4 2.9 reshape.472
  632.1 3.6 reshape.473
  635.9 3.0 copy.286
  641.6 4.2 fusion.74
  649.8 5.1 reshape.470
  654.9 3.7 constant_dynamic-update-slice_fusion.7
  670.0 27.0 %dynamic-update-slice.15 = f32[8,4,131264]{2,1,0:T(4,128)} dynamic-update-slice(f32[8,4,131264]{2,1,0:T(4,128)} %dynamic-update-slice.14, f32[8,4,32768]{2,1,0:T(4,128)} %reshape.477, s32[]{} %constant.184, s32[]{} %constant.184, s32[]{} %constant.191) | dynamic-update-slice | bytes 8388612
  714.5 507.5 %all-reduce.15.cloned.1.call-done = f32[8,4,131264]{2,1,0:T(4,128)} async-done(((f32[8,4,131264]{2,1,0:T(4,128)}), f32[8,4,131264]{2,1,0:T(4,128)}) %all-reduce.15.cloned.1.call-update) | async-done | bytes 16801808
  1222.0 3.3 constant_dynamic-slice_fusion.6
  1233.8 42.6 %all-reduce.13.cloned.1.call-done = f32[1,4,131264]{2,1,0:T(4,128)} async-done(((f32[1,4,131264]{2,1,0:T(4,128)}), f32[1,4,131264]{2,1,0:T(4,128)}) %all-reduce.13.cloned.1.call-update) | async-done | bytes 2100240 | tf_op jit(solution)/shard_map/psum | solution.py:369
  (575 shorter events, 318.0 us)
Async XLA Ops:
  7.2 184.8 %copy-start = (bf16[256,512]{1,0:T(8,128)(2,1)S(1)}, bf16[256,512]{1,0:T(8,128)(2,1)}, u32[]{:S(2)}) copy-start(bf16[256,512]{1,0:T(8,128)(2,1)} %param.31) | copy-start | bytes 786436
  7.2 50.0 %all-gather.6.cloned.1.call-start = ((), (), s32[]{:S(2)}) async-start(), calls=%async_computation.10 | async-start | bytes 1769472 | tf_op jit(solution)/shard_map/all_gather | solution.py:194
  7.9 184.1 %all-gather.8.cloned.1.call-start = ((), (), s32[]{:S(2)}) async-start(), calls=%async_computation.11 | async-start | bytes 1179648 | tf_op jit(solution)/shard_map/all_gather | solution.py:197
  10.0 190.3 %copy-start.14 = (bf16[512,512]{0,1:T(8,128)(2,1)}, bf16[512,512]{0,1:T(8,128)(2,1)S(1)}, u32[]{:S(2)}) copy-start(bf16[512,512]{0,1:T(8,128)(2,1)S(1)} %copy.258) | copy-start | bytes 1572868
  42.3 14.9 %copy-start.83 = (f32[512]{0:T(512)}, f32[512]{0:T(512)S(1)}, u32[]{:S(2)}) copy-start(f32[512]{0:T(512)S(1)} %convert_element_type.224) | copy-start | bytes 6148
  42.3 14.9 %copy-start.66 = (f32[512]{0:T(512)}, f32[512]{0:T(512)S(1)}, u32[]{:S(2)}) copy-start(f32[512]{0:T(512)S(1)} %convert_element_type.223) | copy-start | bytes 6148
  42.5 14.7 %copy-start.58 = (f32[512]{0:T(512)}, f32[512]{0:T(512)S(1)}, u32[]{:S(2)}) copy-start(f32[512]{0:T(512)S(1)} %broadcast_multiply_fusion.8) | copy-start | bytes 6148
  42.6 14.5 %copy-start.68 = (f32[512]{0:T(512)}, f32[512]{0:T(512)S(1)}, u32[]{:S(2)}) copy-start(f32[512]{0:T(512)S(1)} %add_rsqrt_fusion.2) | copy-start | bytes 6148
  62.6 7.1 copy-start.52
  65.3 38.8 %all-to-all-start = ((bf16[512,3,512]{0,1,2:T(4,128)(2,1)}), bf16[512,3,512]{0,1,2:T(4,128)(2,1)S(1)}, u32[]{:S(2)}, u32[]{:S(2)}) async-start(bf16[512,3,512]{0,1,2:T(4,128)(2,1)} %copy.260), calls=%async_computation | async-start | bytes 4194304 | tf_op jit(solution)/shard_map/all_to_all | solution.py:248
  69.0 247.8 %all-gather.10.cloned.1.call-start = ((), (), s32[]{:S(2)}) async-start(), calls=%async_computation.12 | async-start | bytes 2359296 | tf_op jit(solution)/shard_map/all_gather | solution.py:199
  69.7 132.3 %copy-start.74 = (f32[512]{0:T(512)}, f32[512]{0:T(512)S(1)}, u32[]{:S(2)}) copy-start(f32[512]{0:T(512)S(1)} %convert_element_type.228) | copy-start | bytes 6148
  69.7 132.3 %copy-start.60 = (f32[512]{0:T(512)}, f32[512]{0:T(512)S(1)}, u32[]{:S(2)}) copy-start(f32[512]{0:T(512)S(1)} %convert_element_type.227) | copy-start | bytes 6148
  111.0 47.6 %copy-start.53 = (bf16[64,512]{1,0:T(8,128)(2,1)S(1)}, bf16[64,512]{1,0:T(8,128)(2,1)}, u32[]{:S(2)}) copy-start(bf16[64,512]{1,0:T(8,128)(2,1)} %param.36) | copy-start | bytes 196612
  155.1 46.7 %copy-start.5 = (bf16[2048,2,64]{0,2,1:T(8,128)(2,1)}, bf16[2048,2,64]{0,2,1:T(8,128)(2,1)S(1)}, u32[]{:S(2)}) copy-start(bf16[2048,2,64]{0,2,1:T(8,128)(2,1)S(1)} %get-tuple-element.1168) | copy-start | bytes 1572868
  155.1 46.7 %copy-start.12 = (bf16[2048,2,64]{0,2,1:T(8,128)(2,1)}, bf16[2048,2,64]{0,2,1:T(8,128)(2,1)S(1)}, u32[]{:S(2)}) copy-start(bf16[2048,2,64]{0,2,1:T(8,128)(2,1)S(1)} %get-tuple-element.1171) | copy-start | bytes 1572868
  155.1 46.7 %copy-start.51 = (f32[4,2,512]{2,1,0:T(2,128)}, f32[4,2,512]{2,1,0:T(2,128)S(1)}, u32[]{:S(2)}) copy-start(f32[4,2,512]{2,1,0:T(2,128)S(1)} %get-tuple-element.1125) | copy-start | bytes 49156
  155.1 41.0 %all-to-all-start.1 = ((bf16[4,512,128]{1,2,0:T(8,128)(2,1)}), bf16[4,512,128]{1,2,0:T(8,128)(2,1)S(1)}, u32[]{:S(2)}, u32[]{:S(2)}) async-start(bf16[4,512,128]{1,2,0:T(8,128)(2,1)} %copy-done.41), calls=%async_computation.1 | async-start | bytes 1048576 | tf_op jit(solution)/shard_map/all_to_all | solution.py:257
  196.1 17.1 %copy-start.29 = (bf16[4,512,128]{1,2,0:T(8,128)(2,1)}, bf16[4,512,128]{1,2,0:T(8,128)(2,1)S(1)}, u32[]{:S(2)}) copy-start(bf16[4,512,128]{1,2,0:T(8,128)(2,1)S(1)} %all-to-all-done.1) | copy-start | bytes 1572868
  196.1 13.1 %all-to-all-start.3 = ((bf16[256,2,512]{0,1,2:T(2,128)(2,1)}), bf16[256,2,512]{0,1,2:T(2,128)(2,1)}, u32[]{:S(2)}, u32[]{:S(2)}) async-start(bf16[256,2,512]{0,1,2:T(2,128)(2,1)} %copy.267), calls=%async_computation.3 | async-start | bytes 1048576 | tf_op jit(solution)/shard_map/all_to_all | solution.py:249
  201.8 114.2 %copy-start.7 = (f32[512,512]{0,1:T(8,128)}, f32[512,512]{0,1:T(8,128)S(1)}, u32[]{:S(2)}) copy-start(f32[512,512]{0,1:T(8,128)S(1)} %get-tuple-element.729) | copy-start | bytes 3145732
  201.8 12.5 copy-start.55
  202.0 20.2 %copy-start.63 = (f32[512]{0:T(512)}, f32[512]{0:T(512)S(1)}, u32[]{:S(2)}) copy-start(f32[512]{0:T(512)S(1)} %add_rsqrt_fusion.1) | copy-start | bytes 6148
  209.1 12.3 all-to-all-start.2
  212.6 109.3 %all-gather.12.cloned.1.call-start = ((), (), s32[]{:S(2)}) async-start(), calls=%async_computation.13 | async-start | bytes 2359296 | tf_op jit(solution)/shard_map/all_gather | solution.py:201
  223.7 41.5 %copy-start.88 = (bf16[256]{0:T(256)(128)(2,1)S(1)}, bf16[256]{0:T(256)(128)(2,1)}, u32[]{:S(2)}) copy-start(bf16[256]{0:T(256)(128)(2,1)} %param.40) | copy-start | bytes 1540
  223.7 59.8 %copy-start.47 = (bf16[512,512]{1,0:T(8,128)(2,1)S(1)}, bf16[512,512]{1,0:T(8,128)(2,1)}, u32[]{:S(2)}) copy-start(bf16[512,512]{1,0:T(8,128)(2,1)} %param.50) | copy-start | bytes 1572868
  223.7 60.9 %copy-start.54 = (bf16[64,512]{1,0:T(8,128)(2,1)S(1)}, bf16[64,512]{1,0:T(8,128)(2,1)}, u32[]{:S(2)}) copy-start(bf16[64,512]{1,0:T(8,128)(2,1)} %param.38) | copy-start | bytes 196612
  261.0 55.1 %all-to-all-start.4 = ((bf16[4,512,128]{1,2,0:T(8,128)(2,1)}), bf16[4,512,128]{1,2,0:T(8,128)(2,1)S(1)}, u32[]{:S(2)}, u32[]{:S(2)}) async-start(bf16[4,512,128]{1,2,0:T(8,128)(2,1)} %get-tuple-element.225), calls=%async_computation.4 | async-start | bytes 1048576 | tf_op jit(solution)/shard_map/all_to_all | solution.py:268
  265.1 73.7 %copy-start.76 = (f32[512]{0:T(512)}, f32[512]{0:T(512)S(1)}, u32[]{:S(2)}) copy-start(f32[512]{0:T(512)S(1)} %convert_element_type.241) | copy-start | bytes 6148
  265.2 56.8 %copy-start.49 = (f32[512]{0:T(512)}, f32[512]{0:T(512)S(1)}, u32[]{:S(2)}) copy-start(f32[512]{0:T(512)S(1)} %convert_element_type.233) | copy-start | bytes 6148
  283.6 45.3 %copy-start.79 = (f32[8,1,256]{2,1,0:T(1,128)}, f32[8,1,256]{2,1,0:T(1,128)S(1)}, u32[]{:S(2)}) copy-start(f32[8,1,256]{2,1,0:T(1,128)S(1)} %convert_element_type.258) | copy-start | bytes 24580
  284.6 54.2 %copy-start.77 = (f32[512]{0:T(512)}, f32[512]{0:T(512)S(1)}, u32[]{:S(2)}) copy-start(f32[512]{0:T(512)S(1)} %fusion.73) | copy-start | bytes 6148
  316.6 22.3 %copy-start.10 = (f32[512,512]{0,1:T(8,128)}, f32[512,512]{0,1:T(8,128)S(1)}, u32[]{:S(2)}) copy-start(f32[512,512]{0,1:T(8,128)S(1)} %get-tuple-element.731) | copy-start | bytes 3145732
  328.8 10.0 copy-start.70
  342.2 12.4 all-to-all-start.5
  434.0 13.1 %all-to-all-start.6 = ((bf16[4,2,32768]{2,1,0:T(2,128)(2,1)}), bf16[4,2,32768]{2,1,0:T(2,128)(2,1)}, u32[]{:S(2)}, u32[]{:S(2)}) async-start(bf16[4,2,32768]{2,1,0:T(2,128)(2,1)} %reshape.538), calls=%async_computation.6 | async-start | bytes 1048576 | tf_op jit(solution)/shard_map/all_to_all | solution.py:306
  444.9 12.4 copy-start.8
  444.9 12.4 copy-start.56
  444.9 12.4 copy-start.61
  444.9 12.4 copy-start.64
  458.3 8.4 copy-start.11
  458.3 8.4 copy-start.50
  462.5 13.0 %all-to-all-start.7 = ((bf16[512,4,128]{0,2,1:T(8,128)(2,1)}), bf16[512,4,128]{0,2,1:T(8,128)(2,1)}, u32[]{:S(2)}, u32[]{:S(2)}) async-start(bf16[512,4,128]{0,2,1:T(8,128)(2,1)} %bitcast.38), calls=%async_computation.7 | async-start | bytes 1048576 | tf_op jit(solution)/shard_map/all_to_all | solution.py:327
  471.6 11.2 copy-start.6
  471.6 11.2 copy-start.13
  475.5 117.0 %all-to-all-start.9 = ((bf16[1024,2,128]{2,1,0:T(2,128)(2,1)}), bf16[1024,2,128]{2,1,0:T(2,128)(2,1)}, u32[]{:S(2)}, u32[]{:S(2)}) async-start(bf16[1024,2,128]{2,1,0:T(2,128)(2,1)} %copy.289), calls=%async_computation.9 | async-start | bytes 1048576 | tf_op jit(solution)/shard_map/all_to_all | solution.py:307
  581.8 15.3 %copy-start.21 = (f32[512,512]{0,1:T(8,128)S(1)}, f32[512,512]{0,1:T(8,128)}, u32[]{:S(2)}) copy-start(f32[512,512]{0,1:T(8,128)} %copy-done.20) | copy-start | bytes 3145732
  581.8 15.3 %copy-start.32 = (bf16[4,512,128]{1,2,0:T(8,128)(2,1)S(1)}, bf16[4,512,128]{1,2,0:T(8,128)(2,1)}, u32[]{:S(2)}) copy-start(bf16[4,512,128]{1,2,0:T(8,128)(2,1)} %copy-done.31) | copy-start | bytes 1572868
  592.5 43.4 %all-to-all-start.8 = ((bf16[2048,3,128]{2,1,0:T(4,128)(2,1)}), bf16[2048,3,128]{2,1,0:T(4,128)(2,1)}, u32[]{:S(2)}, u32[]{:S(2)}) async-start(bf16[2048,3,128]{2,1,0:T(4,128)(2,1)} %copy.285), calls=%async_computation.8 | async-start | bytes 4194304 | tf_op jit(solution)/shard_map/all_to_all | solution.py:333
  597.0 625.0 %all-reduce.15.cloned.1.call-start = ((), (), s32[]{:S(2)}) async-start(), calls=%async_computation.15 | async-start | bytes 33619968
  605.6 12.9 copy-start.19
  605.6 12.9 copy-start.30
  611.7 11.2 copy-start.9
  611.7 11.2 copy-start.28
  611.7 11.2 copy-start.57
  611.7 11.2 copy-start.62
  611.7 11.2 copy-start.65
  611.7 11.2 copy-start.75
  619.9 7.5 copy-start.34
  714.4 513.0 %copy-start.35 = (bf16[256,2,4,128]{0,3,2,1:T(8,128)(2,1)S(1)}, bf16[256,2,4,128]{0,3,2,1:T(8,128)(2,1)}, u32[]{:S(2)}) copy-start(bf16[256,2,4,128]{0,3,2,1:T(8,128)(2,1)} %copy.291) | copy-start | bytes 1572868
  714.4 561.9 %all-reduce.13.cloned.1.call-start = ((), (), s32[]{:S(2)}) async-start(), calls=%async_computation.14 | async-start | bytes 4202496 | tf_op jit(solution)/shard_map/psum | solution.py:369
  1276.3 7.4 copy-start.39
  1276.3 8.8 slice-start
  (66 other events, 305.1 us)
Sparse Core Ops, SparseCore 0:
  10.2 46.8 all-gather.5
  59.3 42.1 all-gather.7
  103.6 47.2 all-gather.9
  215.3 48.5 all-gather.11
  714.5 507.4 all-reduce.14
  1225.4 50.8 all-reduce.12
where the time goes:
time: 1310 us; the launch traced here: 1300 us
  waiting for transfers between devices  590 us (45%)
  local copies, waits for them, and re-layouts  234 us (18%)
  matrix products  200 us (15%)
  blocking collectives  141 us (11%)
  other arithmetic  65.9 us (5%)
  starting transfers between devices  39.7 us (3%)
  between operations  16.9 us (1%)
    unnamed x7, waiting for transfers between devices  510 us
    unnamed x204, local copies, waits for them, and re-layouts  83.6 us
    psum x1, waiting for transfers between devices, shards(): summed = lax.psum(owned_rows, 'seq')  42.6 us
    dot_general x8, matrix products, one_block(): jnp.einsum('hqk,qhd->khd', recalled.astype(jnp.bfloat16), grad_block, pre...  35.2 us
    all_gather x1, blocking collectives, shards(): lax.all_gather(self_out, 'dp', axis=0, tiled=True)  34.4 us
    all_gather x1, blocking collectives, shards(): lax.all_gather(cross_query, 'dp', axis=0, tiled=True)  33.4 us
    all_gather x1, blocking collectives, shards(): lax.all_gather(cross_out, 'dp', axis=0, tiled=True)  31.5 us
    reshape x16, local copies, waits for them, and re-layouts, shards(): grad_part.reshape(dp_count, seq_count, -1)  29.6 us
  transfers between devices with their start and end apart: 16, of which 8 were waited for; matrix products, arithmetic and copies ran while one was open for 22% of the time, Pallas kernels for 0%

commit v1 on v0

v1 whole, which is shorter than its diff:
```python
import functools
import jax
import jax.numpy as jnp
from jax import lax
from jax.experimental import pallas as pl
from jax.experimental.pallas import tpu as pltpu
from jax.sharding import PartitionSpec as P

bf16 = jnp.bfloat16
f32 = jnp.float32
i32 = jnp.int32
MESH = pl.DeviceIdType.MESH
HD = 64
LANES = 128
epsilon = 1e-05
masked_score = -1e30
gelu_scale = 0.7978845608028654
gelu_cubic = 0.044715
log2_e = 1.4426950408889634


def nn(left, right):
    return jnp.dot(left, right, preferred_element_type=f32)


def nt(left, right, precision=None):
    return lax.dot_general(
        left, right, (((1,), (1,)), ((), ())), preferred_element_type=f32, precision=precision
    )


def tn(left, right):
    return lax.dot_general(
        left, right, (((0,), (0,)), ((), ())), preferred_element_type=f32
    )


def many(count, step):
    if count <= 8:
        for index in range(count):
            step(index)
    else:
        lax.fori_loop(0, count, lambda index, carry: (step(index), carry)[1], 0)


def tiles(rows, size, step):
    lax.fori_loop(0, rows // size, lambda index, carry: (step(pl.ds(pl.multiple_of(index * size, size), size)), carry)[1], 0)


def unit_rows(value):
    average = jnp.mean(value, axis=-1, keepdims=True)
    centred = value - average
    variance = jnp.mean(centred * centred, axis=-1, keepdims=True)
    inverse = lax.rsqrt(variance + epsilon)
    return centred * inverse, inverse


def head_mask(head):
    lane = lax.broadcasted_iota(i32, (1, LANES), 1)
    return (lane < HD) == (head == 0)


def pick(value, mask):
    return jnp.where(mask, value, jnp.zeros_like(value))


def forward_kernel(sizes, *refs):
    dp, sq, rows, mem_rows, width, inner = sizes
    high = dp // 2
    strip = width // dp
    seq_rows = rows * sq
    all_mem = mem_rows * sq
    (len_ref, mlen_ref, hidden_ref, memory_ref, vec_ref, self_in_ref, cross_memory_ref, self_out_ref,
     cross_query_ref, cross_out_ref, ffn_in_ref, ffn_out_ref,
     w_cm, w_so, w_cq, w_co, w_fi, w_fo, vec_full, bias_full, after_self, after_cross, normed_two, cross_q,
     mixed, mem_pair, cross_lse, att_tok, q_all, k_all, v_all, self_lse,
     w_in, hid_all, mem_all, vec_all, normed_all, o_heads,
     loc_sem, hid_s, hid_r, mem_s, mem_r, vec_s, vec_r, in_s, in_r, z_s, z_r, x_s, x_r, c_s, c_r, a_s, a_r) = refs
    me_dp = lax.axis_index("dp")
    me_sq = lax.axis_index("seq")
    me_hi = me_dp // 2
    me_lo = me_dp % 2
    half = me_sq % 2
    pair = me_sq + 1 - 2 * half
    far = (me_sq + 2) % sq
    cross = (pair + 2) % sq
    shards = (cross_memory_ref, self_out_ref, cross_query_ref, cross_out_ref, ffn_in_ref, ffn_out_ref)
    wholes = (w_cm, w_so, w_cq, w_co, w_fi, w_fo)

    def remote(src, dst, send, recv, device):
        return pltpu.make_async_remote_copy(src_ref=src, dst_ref=dst, send_sem=send, recv_sem=recv, device_id=device, device_id_type=MESH)

    def other_dp(step):
        return (me_dp + 1 + step) % dp

    barrier = pltpu.get_barrier_semaphore()
    many(dp - 1, lambda k: pl.semaphore_signal(barrier, inc=1, device_id=(other_dp(k), me_sq), device_id_type=MESH))
    for peer in (pair, far, cross):
        pl.semaphore_signal(barrier, inc=1, device_id=(me_dp, peer), device_id_type=MESH)
    pl.semaphore_wait(barrier, dp - 1 + 3)

    def slab_copy(src, dst_all, slab, send, recv, peer):
        return remote(src, dst_all.at[slab], send, recv.at[slab], (me_dp, peer))

    own_hidden = pltpu.make_async_copy(hidden_ref, hid_all.at[me_sq], loc_sem.at[0])
    own_memory = pltpu.make_async_copy(memory_ref, mem_all.at[me_sq], loc_sem.at[1])
    hid_far = slab_copy(hidden_ref, hid_all, me_sq, hid_s.at[1], hid_r, far)
    hid_pair = slab_copy(hidden_ref, hid_all, me_sq, hid_s.at[0], hid_r, pair)
    mem_far = slab_copy(memory_ref, mem_all, me_sq, mem_s.at[1], mem_r, far)
    mem_pair_copy = slab_copy(memory_ref, mem_all, me_sq, mem_s.at[0], mem_r, pair)
    hid_next = slab_copy(hid_all.at[far], hid_all, far, hid_s.at[2], hid_r, pair)
    mem_next = slab_copy(mem_all.at[far], mem_all, far, mem_s.at[2], mem_r, pair)

    def vec_copy(peer, slot):
        return remote(vec_ref, vec_all.at[slot], vec_s.at[peer], vec_r.at[slot], (peer, me_sq))

    def in_copy(part, peer, slot):
        return remote(
            self_in_ref.at[:, pl.ds(pl.multiple_of(part * width + me_sq * LANES, LANES), LANES)],
            w_in.at[pl.ds(pl.multiple_of(slot * strip, strip), strip), pl.ds(part * LANES, LANES)],
            in_s.at[part, peer], in_r.at[part, slot], (peer, me_sq))

    own_vec = pltpu.make_async_copy(vec_ref, vec_all.at[me_dp], loc_sem.at[2])
    own_in = [pltpu.make_async_copy(
        self_in_ref.at[:, pl.ds(pl.multiple_of(part * width + me_sq * LANES, LANES), LANES)],
        w_in.at[pl.ds(pl.multiple_of(me_dp * strip, strip), strip), pl.ds(part * LANES, LANES)],
        loc_sem.at[3 + part]) for part in range(3)]

    hid_far.start()
    hid_pair.start()
    many(dp - 1, lambda k: vec_copy(other_dp(k), me_dp).start())
    many(dp - 1, lambda k: [in_copy(part, other_dp(k), me_dp).start() for part in range(3)])
    own_hidden.start()
    own_memory.start()
    own_vec.start()
    for copy in own_in:
        copy.start()
    mem_far.start()
    mem_pair_copy.start()

    def columns(index):
        size = shards[index].shape[1] // 2
        return pl.ds(pl.multiple_of(half * size, LANES), size)

    def block_rows(index, slot):
        size = shards[index].shape[0]
        return pl.ds(pl.multiple_of(slot * size, size), size)

    def z_copy(index, peer, slot):
        return remote(shards[index].at[:, columns(index)], wholes[index].at[block_rows(index, slot * 2 + me_lo), columns(index)],
                      z_s.at[index, peer], z_r.at[index, slot], (peer * 2 + me_lo, me_sq))

    def x_copy(index, slot, low, own):
        there = wholes[index].at[block_rows(index, slot * 2 + low), columns(index)]
        src = shards[index].at[:, columns(index)] if own else there
        return remote(src, there, x_s.at[index, slot], x_r.at[index, slot], (me_hi * 2 + 1 - me_lo, me_sq))

    def c_copy(index):
        there = wholes[index].at[:, columns(index)]
        return remote(there, there, c_s.at[index], c_r.at[index], (me_dp, pair))

    def c_wait(index):
        size = shards[index].shape[1] // 2
        there = wholes[index].at[:, pl.ds(pl.multiple_of((1 - half) * size, LANES), size)]
        remote(there, there, c_s.at[index], c_r.at[index], (me_dp, pair)).wait_recv()

    def own_copy(index):
        return pltpu.make_async_copy(shards[index].at[:, columns(index)], wholes[index].at[block_rows(index, me_dp), columns(index)], loc_sem.at[6 + index])

    def other_hi(step):
        return (me_hi + 1 + step) % high

    def first_stage(index):
        many(high - 1, lambda k: z_copy(index, other_hi(k), me_hi).start())
        x_copy(index, me_hi, me_lo, True).start()
        own_copy(index).start()

    def second_stage(index):
        def forward(k):
            z_copy(index, other_hi(k), other_hi(k)).wait_recv()
            x_copy(index, other_hi(k), me_lo, False).start()
        many(high - 1, forward)

    def third_stage(index):
        many(high, lambda k: x_copy(index, k, 1 - me_lo, False).wait_recv())
        own_copy(index).wait()
        c_copy(index).start()

    def finish_weight(index):
        many(high - 1, lambda k: z_copy(index, other_hi(k), me_hi).wait_send())
        many(high, lambda k: x_copy(index, k, me_lo, False).wait_send())
        c_copy(index).wait_send()

    for index in range(6):
        first_stage(index)

    own_vec.wait()
    many(dp - 1, lambda k: vec_copy(other_dp(k), other_dp(k)).wait_recv())
    vec_full[...] = jnp.zeros_like(vec_full)
    bias_full[...] = jnp.zeros_like(bias_full)
    lane_k = lax.broadcasted_iota(i32, (LANES, width), 0)
    lane_j = lax.broadcasted_iota(i32, (LANES, width), 1)
    big = inner // dp
    piece = min(big, LANES)
    big_k = lax.broadcasted_iota(i32, (LANES, inner), 0)
    big_j = lax.broadcasted_iota(i32, (LANES, inner), 1)

    def place(slot):
        hot = ((lane_j - slot * strip == lane_k) & (lane_k < strip)).astype(f32).astype(bf16)
        vec_full[...] = vec_full[...] + nn(vec_all[slot], hot)[:8]
        for part in range(big // piece):
            wide = ((big_j - slot * big - part * piece == big_k) & (big_k < piece)).astype(f32).astype(bf16)
            bias_full[...] = bias_full[...] + nn(vec_all[slot], wide)[8 + part:9 + part]
    lax.fori_loop(0, dp, lambda slot, carry: (place(slot), carry)[1], 0)
    gain_one, shift_one = vec_full[0:1], vec_full[1:2]
    gain_two, shift_two = vec_full[2:3], vec_full[3:4]

    def norm_slab(slab):
        def step(place_rows):
            unit, _ = unit_rows(hid_all[slab, place_rows].astype(f32))
            start = pl.multiple_of(slab * rows + place_rows.start, place_rows.size)
            normed_all[pl.ds(start, place_rows.size)] = (unit * gain_one + shift_one).astype(bf16)
        tiles(rows, 256, step)

    def project_slab(slab):
        def step(place_rows):
            here = pl.ds(pl.multiple_of(slab * rows + place_rows.start, place_rows.size), place_rows.size)
            packed = nn(normed_all[here], w_in[...]).astype(bf16)
            q_all[here] = packed[:, :LANES]
            k_all[here] = packed[:, LANES:2 * LANES]
            v_all[here] = packed[:, 2 * LANES:]
        tiles(rows, 256, step)

    own_hidden.wait()
    norm_slab(me_sq)
    hid_pair_in = slab_copy(hid_all.at[pair], hid_all, pair, hid_s.at[0], hid_r, pair)
    hid_pair_in.wait_recv()
    norm_slab(pair)
    for copy in own_in:
        copy.wait()
    many(dp - 1, lambda k: [in_copy(part, other_dp(k), other_dp(k)).wait_recv() for part in range(3)])
    project_slab(me_sq)
    project_slab(pair)
    slab_copy(hid_all.at[far], hid_all, far, hid_s.at[1], hid_r, far).wait_recv()
    hid_next.start()
    second_stage(0)
    norm_slab(far)
    project_slab(far)
    slab_copy(hid_all.at[cross], hid_all, cross, hid_s.at[2], hid_r, pair).wait_recv()
    norm_slab(cross)
    project_slab(cross)
    slab_copy(mem_all.at[far], mem_all, far, mem_s.at[1], mem_r, far).wait_recv()
    mem_next.start()
    second_stage(1)
    second_stage(2)
    third_stage(0)

    limit = len_ref[0]
    mem_limit = mlen_ref[0]
    scale = HD ** (-0.5) * log2_e

    def softmax_block(scores, values):
        largest = jnp.max(scores, axis=1, keepdims=True)
        powers = jnp.exp2(scores - largest)
        total = jnp.sum(powers, axis=1, keepdims=True)
        return nn(powers.astype(bf16), values) / total, largest + jnp.log2(total)

    def att_copy(block, owner):
        return remote(o_heads.at[pl.ds(pl.multiple_of(block * rows, rows), rows)],
                      att_tok.at[:, pl.ds(pl.multiple_of(owner * LANES, LANES), LANES)],
                      a_s.at[block], a_r.at[owner], (me_dp, block))

    def self_block(block):
        keys = (block + 1) * rows
        here = pl.ds(block * rows, rows)
        query = q_all[here]
        bias = jnp.where(lax.broadcasted_iota(i32, (1, keys), 1) < limit, 0.0, masked_score)
        outs, spreads = [], []
        for head in range(2):
            scores = nt(pick(query, head_mask(head)), k_all[pl.ds(0, keys)]) * scale + bias
            row = lax.broadcasted_iota(i32, (rows, rows), 0)
            column = lax.broadcasted_iota(i32, (rows, rows), 1)
            last = jnp.where(column <= row, scores[:, keys - rows:], masked_score)
            scores = jnp.concatenate([scores[:, :keys - rows], last], axis=1) if block else last
            out, spread = softmax_block(scores, v_all[pl.ds(0, keys)])
            outs.append(out)
            spreads.append(spread)
        o_heads[here] = jnp.where(head_mask(0), outs[0], outs[1]).astype(bf16)
        turned = jnp.transpose(jnp.where(head_mask(0), spreads[0], spreads[1]))
        self_lse[0:1, here] = turned[0:1]
        self_lse[1:2, here] = turned[HD:HD + 1]

        @pl.when(me_sq != block)
        def _():
            att_copy(block, me_sq).start()

    comm_steps = {3: lambda: (third_stage(1), second_stage(3)), 2: lambda: (third_stage(2), second_stage(4)),
                  1: lambda: (third_stage(3), second_stage(5)), 0: lambda: third_stage(4)}
    for block in range(sq - 1, -1, -1):
        self_block(block)
        comm_steps[block]()
    att_tok[:, pl.ds(pl.multiple_of(me_sq * LANES, LANES), LANES)] = o_heads[pl.ds(pl.multiple_of(me_sq * rows, rows), rows)]

    own_memory.wait()
    slab_copy(mem_all.at[pair], mem_all, pair, mem_s.at[0], mem_r, pair).wait_recv()
    slab_copy(mem_all.at[cross], mem_all, cross, mem_s.at[2], mem_r, pair).wait_recv()
    c_wait(0)

    def project_memory(slab, carry):
        mem_pair[pl.ds(pl.multiple_of(slab * mem_rows, mem_rows), mem_rows)] = nn(mem_all[slab], w_cm[...]).astype(bf16)
        return carry
    lax.fori_loop(0, sq, project_memory, 0)

    for peer in (pair, far, cross):
        att_copy(peer, peer).wait_recv()
    c_wait(1)
    c_wait(2)

    def step_two(here):
        value = hidden_ref[here].astype(f32) + nn(att_tok[here], w_so[...])
        after_self[here] = value
        unit, _ = unit_rows(value)
        normed = (unit * gain_two + shift_two).astype(bf16)
        normed_two[here] = normed
        cross_q[here] = nn(normed, w_cq[...]).astype(bf16)
    tiles(rows, 256, step_two)

    mem_bias = jnp.where(lax.broadcasted_iota(i32, (1, all_mem), 1) < mem_limit, 0.0, masked_score)

    def cross_pair(number):
        lanes = pl.ds(number * LANES, LANES)
        query = cross_q[:, lanes]
        outs, spreads = [], []
        for head in range(2):
            scores = nt(pick(query, head_mask(head)), mem_pair[:, lanes]) * scale + mem_bias
            out, spread = softmax_block(scores, mem_pair[:, pl.ds(width + number * LANES, LANES)])
            outs.append(out)
            spreads.append(spread)
        mixed[:, lanes] = jnp.where(head_mask(0), outs[0], outs[1]).astype(bf16)
        turned = jnp.transpose(jnp.where(head_mask(0), spreads[0], spreads[1]))
        cross_lse[2 * number:2 * number + 1] = turned[0:1]
        cross_lse[2 * number + 1:2 * number + 2] = turned[HD:HD + 1]

    for number in range(width // LANES):
        cross_pair(number)
        if number == 1:
            third_stage(5)
    c_wait(3)

    def step_three(here):
        after_cross[here] = after_self[here] + nn(mixed[here], w_co[...])
    tiles(rows, 256, step_three)

    c_wait(4)
    c_wait(5)
    for copy in (hid_far, hid_pair, hid_next, mem_far, mem_pair_copy, mem_next):
        copy.wait_send()
    many(dp - 1, lambda k: vec_copy(other_dp(k), me_dp).wait_send())
    many(dp - 1, lambda k: [in_copy(part, other_dp(k), me_dp).wait_send() for part in range(3)])
    for index in range(6):
        finish_weight(index)
    for peer in (pair, far, cross):
        att_copy(peer, me_sq).wait_send()


def whole_specs(names):
    return [pl.BlockSpec(memory_space=name) for name in names]


def run_forward(sizes, args):
    dp, sq, rows, mem_rows, width, inner = sizes
    seq_rows, all_mem = rows * sq, mem_rows * sq
    high = dp // 2
    V, A, S = pltpu.VMEM, pl.ANY, pltpu.SMEM
    dma = pltpu.SemaphoreType.DMA
    outs = [((width, 2 * width), bf16), ((width, width), bf16), ((width, width), bf16), ((width, width), bf16),
            ((width, inner), bf16), ((inner, width), bf16), ((8, width), f32), ((1, inner), f32),
            ((rows, width), f32), ((rows, width), f32), ((rows, width), bf16), ((rows, width), bf16),
            ((rows, width), bf16), ((all_mem, 2 * width), bf16), ((8, rows), f32), ((rows, width), bf16),
            ((seq_rows, LANES), bf16), ((seq_rows, LANES), bf16), ((seq_rows, LANES), bf16), ((8, seq_rows), f32)]
    scratch = [pltpu.VMEM((width, 3 * LANES), bf16), pltpu.VMEM((sq, rows, width), bf16), pltpu.VMEM((sq, mem_rows, width), bf16),
               pltpu.VMEM((dp, 16, LANES), bf16), pltpu.VMEM((seq_rows, width), bf16), pltpu.VMEM((seq_rows, LANES), bf16),
               dma((12,)), dma((3,)), dma((sq,)), dma((3,)), dma((sq,)), dma((dp,)), dma((dp,)), dma((3, dp)), dma((3, dp)),
               dma((6, high)), dma((6, high)), dma((6, high)), dma((6, high)), dma((6,)), dma((6,)), dma((sq,)), dma((sq,))]
    return pl.pallas_call(
        functools.partial(forward_kernel, sizes),
        out_shape=[jax.ShapeDtypeStruct(*out) for out in outs],
        in_specs=whole_specs([S, S, V, V, V, A, A, A, A, A, A, A]),
        out_specs=whole_specs([V] * len(outs)),
        scratch_shapes=scratch,
        compiler_params=pltpu.CompilerParams(collective_id=0, has_side_effects=True, vmem_limit_bytes=60 << 20),
        name="forward",
    )(*args)


def shards(hidden_in, memory, lengths, memory_lengths, self_in, self_out, cross_query, cross_memory, cross_out,
           ffn_in, ffn_bias, ffn_out, out_bias, gain_self, shift_self, gain_cross, shift_cross, gain_ffn, shift_ffn,
           exit_weight, grad_result, grad_halting):
    dp = lax.axis_size("dp")
    sq = lax.axis_size("seq")
    rows, width = hidden_in.shape
    mem_rows = memory.shape[0]
    inner = ffn_in.shape[1]
    sizes = (dp, sq, rows, mem_rows, width, inner)
    strip = width // dp
    big = inner // dp
    piece = min(big, LANES)
    vectors = jnp.stack([gain_self, shift_self, gain_cross, shift_cross, gain_ffn, shift_ffn, out_bias, exit_weight])
    packed_vec = jnp.concatenate([
        jnp.pad(vectors, ((0, 0), (0, LANES - strip))),
        jnp.pad(ffn_bias.reshape(big // piece, piece), ((0, 8 - big // piece), (0, LANES - piece)))])
    (w_cm, w_so, w_cq, w_co, w_fi, w_fo, vec_full, bias_full, after_self, after_cross, normed_two, cross_q,
     mixed, mem_pair, cross_lse, att_tok, q_all, k_all, v_all, self_lse) = run_forward(
        sizes, (lengths, memory_lengths, hidden_in, memory, packed_vec, self_in, cross_memory, self_out, cross_query, cross_out, ffn_in, ffn_out))
    return finish(locals())


def old_norm(value, gain, shift):
    average = jnp.mean(value, axis=-1, keepdims=True)
    centred = value - average
    variance = jnp.mean(centred * centred, axis=-1, keepdims=True)
    inverse = lax.rsqrt(variance + epsilon)
    unit = centred * inverse
    return (unit * gain + shift, unit, inverse)


def old_norm_back(grad_out, unit, inverse, gain):
    scaled = grad_out * gain
    first_mean = jnp.mean(scaled, axis=-1, keepdims=True)
    second_mean = jnp.mean(scaled * unit, axis=-1, keepdims=True)
    grad_in = inverse * (scaled - first_mean - unit * second_mean)
    return (grad_in, jnp.sum(grad_out * unit, axis=0), jnp.sum(grad_out, axis=0))


def old_attend_back(queries, keys_in, values_in, spread, grad_mixed, key_limit, causal):
    query_rows, model_width = queries.shape
    heads = model_width // HD
    block_rows = min(512, query_rows)
    key_rows = keys_in.shape[0]
    key_heads = keys_in.reshape(key_rows, heads, HD)
    value_heads = values_in.reshape(key_rows, heads, HD)
    scale = HD ** (-0.5)

    def one_block(running, items):
        grad_keys, grad_values = running
        index, block_spread = items
        first = index * block_rows
        query = lax.dynamic_slice_in_dim(queries, first, block_rows, 0).reshape(block_rows, heads, HD)
        grad = lax.dynamic_slice_in_dim(grad_mixed, first, block_rows, 0).reshape(block_rows, heads, HD)
        scores = jnp.einsum("qhd,khd->hqk", query, key_heads, preferred_element_type=f32) * scale
        place = jnp.arange(key_rows)
        allowed = place[None, :] < key_limit
        if causal:
            allowed = allowed & (place[None, :] <= first + jnp.arange(block_rows)[:, None])
        scores = jnp.where(allowed[None], scores, masked_score)
        recalled = jnp.exp(scores - block_spread[:, :, None])
        grad_probs = jnp.einsum("qhd,khd->hqk", grad, value_heads, preferred_element_type=f32)
        weighted = jnp.sum(recalled * grad_probs, axis=-1, keepdims=True)
        grad_scores = (recalled * (grad_probs - weighted)).astype(bf16)
        grad_query = jnp.einsum("hqk,khd->qhd", grad_scores, key_heads, preferred_element_type=f32) * scale
        grad_keys = grad_keys + jnp.einsum("hqk,qhd->khd", grad_scores, query, preferred_element_type=f32) * scale
        grad_values = grad_values + jnp.einsum("hqk,qhd->khd", recalled.astype(bf16), grad, preferred_element_type=f32)
        return (grad_keys, grad_values), grad_query.reshape(block_rows, model_width).astype(bf16)

    zero = jnp.zeros((key_rows, heads, HD), f32)
    (grad_keys, grad_values), grad_queries = lax.scan(one_block, (zero, zero), (jnp.arange(query_rows // block_rows), spread))
    return grad_queries.reshape(query_rows, model_width), grad_keys.reshape(key_rows, model_width), grad_values.reshape(key_rows, model_width)


def finish(env):
    class E: pass
    e = E(); e.__dict__.update(env)
    dp, sq, rows, width, mem_rows = e.dp, e.sq, e.rows, e.width, e.mem_rows
    joint = lax.all_gather(e.self_in, "dp", axis=0, tiled=True)
    gain_one, shift_one, gain_two, shift_two, gain_three, shift_three, outer_bias, exit_col = [e.vec_full[i] for i in range(8)]
    positions = lax.axis_index("seq") * rows + jnp.arange(rows)
    live = (positions < e.lengths[0]).astype(f32)
    hidden = e.hidden_in.astype(f32)
    n1, unit_one, inv_one = old_norm(hidden, gain_one, shift_one)
    n1 = n1.astype(bf16)
    _, unit_two, inv_two = old_norm(e.after_self, gain_two, shift_two)
    n3, unit_three, inv_three = old_norm(e.after_cross, gain_three, shift_three)
    n3 = n3.astype(bf16)
    inner_pre = nn(n3, e.w_fi) + e.bias_full[0]
    bent = jnp.tanh(gelu_scale * (inner_pre + gelu_cubic * inner_pre ** 3))
    active = (0.5 * inner_pre * (1.0 + bent)).astype(bf16)
    slope = 0.5 * (1.0 + bent) + 0.5 * inner_pre * (1.0 - bent * bent) * gelu_scale * (1.0 + 3.0 * gelu_cubic * inner_pre * inner_pre)
    output = e.after_cross + nn(active, e.w_fo) + outer_bias
    halting = jax.nn.sigmoid(jnp.dot(output, exit_col, precision=lax.Precision.HIGHEST))
    grad_logit = e.grad_halting * live * halting * (1.0 - halting)
    grad_exit = jnp.dot(grad_logit, output, precision=lax.Precision.HIGHEST)
    grad_output = e.grad_result.astype(f32) * live[:, None] + grad_logit[:, None] * exit_col[None, :]
    gb = grad_output.astype(bf16)
    g_ob = jnp.sum(gb.astype(f32), axis=0)
    g_fo = tn(active, gb)
    g_inner = (nt(gb, e.w_fo) * slope).astype(bf16)
    g_fb = jnp.sum(g_inner.astype(f32), axis=0)
    g_fi = tn(n3, g_inner)
    gn3, gg3, gs3 = old_norm_back(nt(g_inner, e.w_fi), unit_three, inv_three, gain_three)
    gcr = grad_output + gn3
    gcb = gcr.astype(bf16)
    g_co = tn(e.mixed, gcb)
    gmix = nt(gcb, e.w_co).astype(bf16)
    spread_cross = (e.cross_lse * (1 / log2_e))[None]
    gcq, gmk, gmv = old_attend_back(e.cross_q, e.mem_pair[:, :width], e.mem_pair[:, width:], spread_cross, gmix, e.memory_lengths[0], False)
    gmp = lax.psum_scatter(jnp.concatenate([gmk, gmv], axis=1), "seq", scatter_dimension=0, tiled=True).astype(bf16)
    g_cq = tn(e.normed_two, gcq)
    g_cm = tn(e.memory, gmp)
    grad_memory = nt(gmp, e.w_cm)
    gn2, gg2, gs2 = old_norm_back(nt(gcq, e.w_cq), unit_two, inv_two, gain_two)
    gsr = gcr + gn2
    gsb = gsr.astype(bf16)
    g_so = tn(e.att_tok, gsb)
    gatt = nt(gsb, e.w_so).astype(bf16)
    gatt_heads = lax.all_to_all(gatt, "seq", split_axis=1, concat_axis=0, tiled=True)
    spread_self = (e.self_lse[:2] * (1 / log2_e)).reshape(2, sq, rows).transpose(1, 0, 2)
    gq, gk, gv = old_attend_back(e.q_all, e.k_all, e.v_all, spread_self, gatt_heads, e.lengths[0], True)
    gp = lax.all_to_all(jnp.stack([gq, gk.astype(bf16), gv.astype(bf16)], axis=1), "seq", split_axis=0, concat_axis=2, tiled=True).reshape(rows, 3 * width)
    g_si = tn(n1, gp)
    gn1, gg1, gs1 = old_norm_back(nt(gp, joint), unit_one, inv_one, gain_one)
    grad_hidden = gsr + gn1
    grads = (g_si, g_so, g_cq, g_cm, g_co, g_fi, g_fb, g_fo, g_ob, gg1, gs1, gg2, gs2, gg3, gs3, grad_exit)
    pieces = [None] * len(grads)
    for i, g in enumerate(grads):
        if g.ndim == 2:
            part = lax.psum_scatter(g.astype(bf16), "dp", scatter_dimension=0, tiled=True)
            pieces[i] = lax.psum(part.astype(f32), "seq")
    small = [i for i, g in enumerate(grads) if g.ndim == 1]
    flat = jnp.concatenate([grads[i].reshape(dp, -1) for i in small], axis=1)
    flat = lax.dynamic_slice_in_dim(lax.psum(flat, ("dp", "seq")), lax.axis_index("dp"), 1, 0)[0]
    offset = 0
    for i in small:
        n = grads[i].size // dp
        pieces[i] = flat[offset:offset + n]
        offset += n
    return (output.astype(bf16), halting, grad_hidden, grad_memory) + tuple(pieces)


def solution(mesh):
    both = P(("dp", "seq"), None)
    matrix = P("dp", None)
    vector = P("dp")
    return jax.shard_map(
        shards,
        mesh=mesh,
        in_specs=(both, both, vector, vector, matrix, matrix, matrix, matrix, matrix, matrix, vector, matrix)
        + (vector,) * 8 + (both, P(("dp", "seq"))),
        out_specs=(both, P(("dp", "seq")), both, both) + (matrix,) * 6 + (vector, matrix) + (vector,) * 8,
        check_vma=False,
    )
```

time: 1310 us -> 784 us (0.60)
  waiting for transfers between devices: 590 us -> 354 us
  local copies, waits for them, and re-layouts: 234 us -> 62 us
  matrix products: 200 us -> 122 us
  Pallas kernels: 0 us -> 77.5 us
  blocking collectives: 141 us -> 86.3 us
  starting transfers between devices: 39.7 us -> 8.95 us
  other arithmetic: 65.9 us -> 42.8 us
    unnamed x7 -> x10, waiting for transfers between devices: 510 us -> 64.4 us
    reduce_scatter x0 -> x7, waiting for transfers between devices: none -> 213 us  [the longest x6 213 us: finish(): lax.psum_scatter(g.astype(bf16), 'dp', scatter_dimension=0, tiled=True)]
    all_gather x4 -> x0, blocking collectives: 118 us -> none  [the longest x1 34.4 us: shards(): lax.all_gather(self_out, 'dp', axis=0, tiled=True)]
    psum x0 -> x2, blocking collectives: none -> 86.3 us  [the longest x1 45.9 us: finish(): pieces[i] = lax.psum(part.astype(f32), 'seq')]
    dot_general x71 -> x38, matrix products: 188 us -> 109 us  [the longest x5 25 us: one_block(): jnp.einsum('hqk,qhd->khd', recalled.astype(bf16), grad, preferred_element...]
    pallas_call x0 -> x1, Pallas kernels: none -> 77.5 us  [run_forward(): pl.pallas_call(functools.partial(forward_kernel, sizes), out_shape=[jax.S...]
    unnamed x204 -> x97, local copies, waits for them, and re-layouts: 83.6 us -> 9.32 us
    psum x1 -> x0, waiting for transfers between devices: 42.6 us -> none  [shards(): summed = lax.psum(owned_rows, 'seq')]
  transfers between devices with their start and end apart: 16 -> 11, of which waited for: 8 -> 8; matrix products, arithmetic and copies ran while one was open for 22% -> 20% of each run, Pallas kernels for 0% -> 0%
where the time goes in v1:
time: 784 us; the launch traced here: 773 us
  waiting for transfers between devices  354 us (45%)
  matrix products  122 us (16%)
  blocking collectives  86.3 us (11%)
  Pallas kernels  77.5 us (10%)
  local copies, waits for them, and re-layouts  62 us (8%)
  other arithmetic  42.8 us (5%)
  between operations  16 us (2%)
  starting transfers between devices  8.95 us (1%)
    reduce_scatter x6, waiting for transfers between devices, finish(): lax.psum_scatter(g.astype(bf16), 'dp', scatter_dimension=0, tiled=True)  213 us
    pallas_call x1, Pallas kernels, run_forward(): pl.pallas_call(functools.partial(forward_kernel, sizes), out_shape=[jax.S...  77.5 us
    unnamed x10, waiting for transfers between devices  64.4 us
    psum x1, blocking collectives, finish(): pieces[i] = lax.psum(part.astype(f32), 'seq')  45.9 us
    all_gather x1, waiting for transfers between devices, finish(): joint = lax.all_gather(e.self_in, 'dp', axis=0, tiled=True)  45.3 us
    psum x1, blocking collectives, finish(): lax.psum(flat, ('dp', 'seq'))  40.4 us
    all_to_all x1, waiting for transfers between devices, finish(): lax.all_to_all(jnp.stack([gq, gk.astype(bf16), gv.astype(bf16)], axis=1),...  25.2 us
    dot_general x5, matrix products, one_block(): jnp.einsum('hqk,qhd->khd', recalled.astype(bf16), grad, preferred_element...  25 us
  transfers between devices with their start and end apart: 11, of which 8 were waited for; matrix products, arithmetic and copies ran while one was open for 20% of the time, Pallas kernels for 0%

profile of v1, /device:TPU:0, one launch (start us, length us, event | category | flops | bytes accessed | tf_op | source)
XLA Modules:
  0.0 773.5 jit_solution(15899501582965449522)
XLA Ops:
  11.1 77.5 %forward.1 = (bf16[512,1024]{1,0:T(8,128)(2,1)}, bf16[512,512]{1,0:T(8,128)(2,1)}, bf16[512,512]{1,0:T(8,128)(2,1)}, bf16[512,512]{1,0:T(8,128)(2,1)}, bf16[512,...) custom-call(s32[1]{0:T(128)} %copy.146.refs_0_, ...), custom_call_target="tpu_custom_call" | custom-call | tf_op jit(solution)/shard_map/forward/pallas_call | solution.py:385
  90.0 1.5 multiply_reduce_fusion.7
  91.5 1.6 fusion.68
  94.4 2.0 copy.93
  96.5 2.7 fusion.67
  99.2 2.3 copy.94
  101.5 1.5 copy.92
  103.1 3.1 fusion.64
  106.2 2.4 fusion.69
  111.2 6.7 convert_reduce_fusion
  119.3 2.1 multiply_reduce_fusion.2
  122.9 2.4 fusion.71
  125.3 10.8 %multiply_reduce_fusion.1 = (f32[8,512]{1,0:T(8,128)S(1)}, f32[8,512,1024]{2,1,0:T(8,128)}) fusion(f32[8,512,1024]{2,1,0:T(8,128)S(1)} %fusion.71, f32[8,512]{1,0:T(8,128)} %broadcast_multiply_fusion, bf16[512,8,64]{0,2,1:T(8,128)(2,1)} %bitcast.180, bf16[1024,8,64]{0,2,1:T(8,128)(2,1)} %bitcast.173, pred[1024]{0:T(1024)(128)(4,1)} %iota_compare_fusion.4), kind=kOutput, calls=%fused_computation.24 | convolution fusion | flops 557838336 | bytes 35161088 | tf_op jit(solution)/shard_map/while/body/eval_jaxpr/qhd,khd->hqk/dot_general | solution.py:450
  136.1 7.3 fusion.16
  143.5 7.0 multiply_convert_fusion.1
  150.5 1.6 convolution_multiply_fusion.2
  152.1 1.6 copy-done
  153.7 2.5 pad_maximum_fusion
  158.6 7.6 fusion.29
  168.0 2.5 multiply_reduce_fusion.3
  170.5 2.0 multiply_add_fusion
  174.5 5.8 convolution_convert_fusion.1
  180.4 2.3 convolution_convert_fusion.7
  182.7 4.1 all-to-all-start
  186.9 4.4 convolution_convert_fusion.2
  193.9 1.5 slice_multiply_fusion
  195.3 6.4 all-to-all-done
  201.7 1.9 copy.114
  204.1 82.2 %while.3 = (s32[]{:T(128)}, f32[2048,2,64]{0,2,1:T(8,128)S(1)}, f32[2048,2,64]{0,2,1:T(8,128)}, bf16[4,512,128]{2,1,0:T(8,128)(2,1)}, s32[4]{0:T(128)}, /*index=...) while((s32[]{:T(128)}, f32[2048,2,64]{0,2,1:T(8,128)S(1)}, ...), condition=%wide.region_13.14_spmd.clone, body=%wide.region_11.13_spmd.clone.sunk | while | flops 1377175040 | bytes 74879216 | solution.py:466
  211.8 3.5 fusion.141
  215.3 3.0 multiply_reduce_fusion.12
  218.4 2.6 multiply_convert_fusion.6
  220.9 1.4 fusion.142
  231.3 4.7 fusion.141
  236.1 3.0 multiply_reduce_fusion.12
  239.1 2.6 multiply_convert_fusion.6
  252.1 4.7 fusion.141
  256.8 3.0 multiply_reduce_fusion.12
  259.8 2.6 multiply_convert_fusion.6
  262.4 1.4 fusion.142
  272.8 4.7 fusion.141
  277.5 3.0 multiply_reduce_fusion.12
  280.6 2.6 multiply_convert_fusion.6
  283.1 1.4 fusion.142
  289.7 1.5 pad_maximum_fusion.1
  291.2 10.9 %copy.103 = bf16[2048,3,128]{2,1,0:T(4,128)(2,1)} copy(bf16[2048,3,128]{2,0,1:T(8,128)(2,1)S(1)} %pad_maximum_fusion.1) | data formatting | bytes 3145728 | tf_op jit(solution)/shard_map/stack | solution.py:518
  302.1 4.4 all-to-all-start.1
  307.1 25.2 %all-to-all-done.1 = bf16[2048,3,128]{2,1,0:T(4,128)(2,1)} async-done(((bf16[2048,3,128]{2,1,0:T(4,128)(2,1)}), bf16[2048,3,128]{2,1,0:T(4,128)(2,1)}, u32[]{:S(2)}, u32[]{:S(2)}) %all-to-all-start.1) | async-done | bytes 1572896 | tf_op jit(solution)/shard_map/all_to_all | solution.py:518
  332.3 1.8 copy.104
  334.1 1.6 copy.105
  335.7 3.9 convolution_convert_fusion
  339.8 2.7 fusion.27
  342.5 2.3 copy.107
  345.9 53.7 %reduce-scatter.15.cloned.1.call-done = bf16[64,512]{1,0:T(8,128)(2,1)} async-done(((bf16[512,512]{1,0:T(8,128)(2,1)}), bf16[64,512]{1,0:T(8,128)(2,1)}) %reduce-scatter.15.cloned.1.call-update) | async-done | bytes 65552 | tf_op jit(solution)/shard_map/reduce_scatter | solution.py:526
  399.6 45.3 %all-gather.2.cloned.1.call-done = bf16[512,1536]{1,0:T(8,128)(2,1)} async-done(((bf16[64,1536]{1,0:T(8,128)(2,1)}), bf16[512,1536]{1,0:T(8,128)(2,1)}) %all-gather.2.cloned.1.call-update) | async-done | bytes 1572880 | tf_op jit(solution)/shard_map/all_gather | solution.py:474
  444.8 4.0 fusion.42
  449.1 40.4 %psum.62 = f32[8,768]{1,0:T(8,128)S(1)} all-reduce(f32[8,768]{1,0:T(8,128)S(1)} %concatenate.11), channel_id=1, replica_groups=mesh['dp'=8,'seq'=4] {'dp','seq'}, use_global_device_ids=true, to_apply=%region_37.38 | all-reduce | flops 6144 | bytes 49152 | tf_op jit(solution)/shard_map/psum | solution.py:530
  490.7 2.6 fusion.39
  493.3 21.6 %reduce-scatter.23.cloned.1.call-done = bf16[256,512]{1,0:T(8,128)(2,1)} async-done(((bf16[2048,512]{1,0:T(8,128)(2,1)}), bf16[256,512]{1,0:T(8,128)(2,1)}) %reduce-scatter.23.cloned.1.call-update) | async-done | bytes 262160 | tf_op jit(solution)/shard_map/reduce_scatter | solution.py:526
  514.9 70.3 %reduce-scatter.21.cloned.1.call-done = bf16[64,2048]{1,0:T(8,128)(2,1)} async-done(((bf16[512,2048]{1,0:T(8,128)(2,1)}), bf16[64,2048]{1,0:T(8,128)(2,1)}) %reduce-scatter.21.cloned.1.call-update) | async-done | bytes 262160 | tf_op jit(solution)/shard_map/reduce_scatter | solution.py:526
  585.2 67.3 %reduce-scatter.13.cloned.1.call-done = bf16[64,1536]{1,0:T(8,128)(2,1)} async-done(((bf16[512,1536]{1,0:T(8,128)(2,1)}), bf16[64,1536]{1,0:T(8,128)(2,1)}) %reduce-scatter.13.cloned.1.call-update) | async-done | bytes 196624 | tf_op jit(solution)/shard_map/reduce_scatter | solution.py:526
  652.5 2.5 fusion.51
  655.1 63.7 %reduce-scatter.25.cloned.1.call-done = bf16[64,1024]{1,0:T(8,128)(2,1)} async-done(((bf16[512,1024]{1,0:T(8,128)(2,1)}), bf16[64,1024]{1,0:T(8,128)(2,1)}) %reduce-scatter.25.cloned.1.call-update) | async-done | bytes 131088
  719.9 45.9 %all-reduce.4 = (f32[64,1536]{1,0:T(8,128)}, f32[64,512]{1,0:T(8,128)}, f32[64,512]{1,0:T(8,128)}, f32[64,1024]{0,1:T(8,128)S(1)}, f32[64,512]{1,0:T(8,128)}, /*index=5*/f32[64,2048]{1,0:T(8,128)}, f32[256,512]{1,0:T(8,128)}) all-reduce(bf16[64,1536]{1,0:T(8,128)(2,1)} %reduce-scatter.13.cloned.1.call-do, ...), channel_id=1, replica_groups=mesh['dp'=8,'seq'=4] {'seq'}, use_global_device_ids=true, to_apply=%region_18.19 | all-reduce | flops 524288 | bytes 3145728 | tf_op jit(solution)/shard_map/psum | solution.py:527
  (216 shorter events, 63.0 us)
Async XLA Ops:
  7.2 332.6 %reduce-scatter.11.cloned.1.call-start = ((), (), s32[]{:S(2)}) async-start(), calls=%async_computation.11 | async-start | bytes 5242880 | tf_op jit(solution)/shard_map/reduce_scatter | solution.py:506
  93.1 10.0 %copy-start.25 = (f32[1,512]{1,0:T(1,128)}, f32[1,512]{1,0:T(1,128)S(1)}, u32[]{:S(2)}) copy-start(f32[1,512]{1,0:T(1,128)S(1)} %get-tuple-element.405) | copy-start | bytes 6148
  93.1 28.3 %copy-start.23 = (f32[1,512]{1,0:T(1,128)}, f32[1,512]{1,0:T(1,128)S(1)}, u32[]{:S(2)}) copy-start(f32[1,512]{1,0:T(1,128)S(1)} %get-tuple-element.406) | copy-start | bytes 6148
  93.1 28.3 %copy-start.30 = (f32[1,512]{1,0:T(1,128)}, f32[1,512]{1,0:T(1,128)S(1)}, u32[]{:S(2)}) copy-start(f32[1,512]{1,0:T(1,128)S(1)} %get-tuple-element.403) | copy-start | bytes 6148
  96.5 6.6 copy-start.1
  103.0 3.1 copy-start.43
  103.0 3.1 copy-start.44
  106.1 2.5 copy-start.7
  106.2 3.4 copy-start.22
  106.2 4.4 copy-start.42
  106.2 5.0 copy-start.13
  108.6 1.0 copy-start.9
  110.6 10.8 %copy-start.34 = (f32[512]{0:T(512)}, f32[512]{0:T(512)S(1)}, u32[]{:S(2)}) copy-start(f32[512]{0:T(512)S(1)} %fusion.62) | copy-start | bytes 6148
  111.2 10.1 %copy-start.27 = (f32[512]{0:T(512)}, f32[512]{0:T(512)S(1)}, u32[]{:S(2)}) copy-start(f32[512]{0:T(512)S(1)} %get-tuple-element.384) | copy-start | bytes 6148
  111.2 8.1 %copy-start.11 = (bf16[512,2048]{1,0:T(8,128)(2,1)S(1)}, bf16[512,2048]{1,0:T(8,128)(2,1)}, u32[]{:S(2)}) copy-start(bf16[512,2048]{1,0:T(8,128)(2,1)} %get-tuple-element.131) | copy-start | bytes 6291460
  118.0 1.3 copy-start.46
  119.3 3.1 copy-start.18
  121.3 1.6 copy-start.5
  122.4 33.9 %copy-start.2 = (f32[512,512]{1,0:T(8,128)}, f32[512,512]{1,0:T(8,128)S(1)}, u32[]{:S(2)}) copy-start(f32[512,512]{1,0:T(8,128)S(1)} %get-tuple-element.391) | copy-start | bytes 3145732
  143.5 7.0 copy-start.6
  150.5 3.2 copy-start
  156.2 1.0 copy-start.17
  156.3 189.6 %reduce-scatter.19.cloned.1.call-start = ((), (), s32[]{:S(2)}) async-start(), calls=%async_computation.15 | async-start | bytes 589824 | tf_op jit(solution)/shard_map/reduce_scatter | solution.py:526
  158.5 7.7 copy-start.15
  158.6 9.0 %copy-start.3 = (f32[512,512]{1,0:T(8,128)S(1)}, f32[512,512]{1,0:T(8,128)}, u32[]{:S(2)}) copy-start(f32[512,512]{1,0:T(8,128)} %get-tuple-element.134) | copy-start | bytes 3145732
  158.6 187.3 %reduce-scatter.17.cloned.1.call-start = ((), (), s32[]{:S(2)}) async-start(), calls=%async_computation.14 | async-start | bytes 589824 | tf_op jit(solution)/shard_map/reduce_scatter | solution.py:526
  166.2 1.8 copy-start.32
  167.5 232.1 %reduce-scatter.15.cloned.1.call-start = ((), (), s32[]{:S(2)}) async-start(), calls=%async_computation.13 | async-start | bytes 589824 | tf_op jit(solution)/shard_map/reduce_scatter | solution.py:526
  167.7 4.8 copy-start.16
  170.5 4.0 copy-start.14
  170.5 4.0 copy-start.28
  170.5 4.0 copy-start.31
  170.5 4.0 copy-start.35
  170.5 4.0 copy-start.45
  173.8 271.0 %all-gather.2.cloned.1.call-start = ((), (), s32[]{:S(2)}) async-start(), calls=%async_computation.10 | async-start | bytes 1769472 | tf_op jit(solution)/shard_map/all_gather | solution.py:474
  174.4 340.5 %reduce-scatter.23.cloned.1.call-start = ((), (), s32[]{:S(2)}) async-start(), calls=%async_computation.17 | async-start | bytes 2359296 | tf_op jit(solution)/shard_map/reduce_scatter | solution.py:526
  180.4 6.5 copy-start.24
  180.4 6.6 copy-start.26
  182.7 19.0 %all-to-all-start = ((bf16[512,4,128]{0,2,1:T(8,128)(2,1)}), bf16[512,4,128]{0,2,1:T(8,128)(2,1)}, u32[]{:S(2)}, u32[]{:S(2)}) async-start(bf16[512,4,128]{0,2,1:T(8,128)(2,1)} %bitcast.28), calls=%async_computation | async-start | bytes 1048576 | tf_op jit(solution)/shard_map/all_to_all | solution.py:515
  186.9 398.3 %reduce-scatter.21.cloned.1.call-start = ((), (), s32[]{:S(2)}) async-start(), calls=%async_computation.16 | async-start | bytes 2359296 | tf_op jit(solution)/shard_map/reduce_scatter | solution.py:526
  291.2 15.4 %copy-start.4 = (bf16[512,512]{1,0:T(8,128)(2,1)S(1)}, bf16[512,512]{1,0:T(8,128)(2,1)}, u32[]{:S(2)}) copy-start(bf16[512,512]{1,0:T(8,128)(2,1)} %refs_2_.1) | copy-start | bytes 1572868
  302.1 30.2 %all-to-all-start.1 = ((bf16[2048,3,128]{2,1,0:T(4,128)(2,1)}), bf16[2048,3,128]{2,1,0:T(4,128)(2,1)}, u32[]{:S(2)}, u32[]{:S(2)}) async-start(bf16[2048,3,128]{2,1,0:T(4,128)(2,1)} %copy.103), calls=%async_computation.1 | async-start | bytes 4194304 | tf_op jit(solution)/shard_map/all_to_all | solution.py:518
  306.5 29.2 %copy-start.29 = (f32[1,512]{1,0:T(1,128)S(1)}, f32[1,512]{1,0:T(1,128)}, u32[]{:S(2)}) copy-start(f32[1,512]{1,0:T(1,128)} %get-tuple-element.401) | copy-start | bytes 6148
  306.6 29.2 %copy-start.37 = (f32[1,512]{1,0:T(1,128)S(1)}, f32[1,512]{1,0:T(1,128)}, u32[]{:S(2)}) copy-start(f32[1,512]{1,0:T(1,128)} %get-tuple-element.400) | copy-start | bytes 6148
  306.6 346.0 %reduce-scatter.13.cloned.1.call-start = ((), (), s32[]{:S(2)}) async-start(), calls=%async_computation.12 | async-start | bytes 1769472 | tf_op jit(solution)/shard_map/reduce_scatter | solution.py:526
  335.7 4.1 copy-start.12
  339.6 5.2 copy-start.10
  339.6 5.8 copy-start.36
  339.6 5.9 copy-start.39
  339.6 5.9 copy-start.38
  339.6 6.0 copy-start.33
  339.7 6.1 copy-start.41
  339.7 6.1 copy-start.40
  339.7 379.1 %reduce-scatter.25.cloned.1.call-start = ((), (), s32[]{:S(2)}) async-start(), calls=%async_computation.18 | async-start | bytes 1179648
  448.9 203.7 %copy-start.8 = (f32[256,1024]{0,1:T(8,128)S(1)}, f32[256,1024]{0,1:T(8,128)}, u32[]{:S(2)}) copy-start(f32[256,1024]{0,1:T(8,128)} %reduce-scatter.11.cloned.1.call-done) | copy-start | bytes 3145732
  448.9 271.0 %copy-start.19 = (bf16[64,512]{1,0:T(8,128)(2,1)S(1)}, bf16[64,512]{1,0:T(8,128)(2,1)}, u32[]{:S(2)}) copy-start(bf16[64,512]{1,0:T(8,128)(2,1)} %reduce-scatter.19.cloned.1.call-done) | copy-start | bytes 196612
  448.9 271.0 %copy-start.20 = (bf16[64,512]{1,0:T(8,128)(2,1)S(1)}, bf16[64,512]{1,0:T(8,128)(2,1)}, u32[]{:S(2)}) copy-start(bf16[64,512]{1,0:T(8,128)(2,1)} %reduce-scatter.17.cloned.1.call-done) | copy-start | bytes 196612
  448.9 271.0 %copy-start.21 = (bf16[64,512]{1,0:T(8,128)(2,1)S(1)}, bf16[64,512]{1,0:T(8,128)(2,1)}, u32[]{:S(2)}) copy-start(bf16[64,512]{1,0:T(8,128)(2,1)} %reduce-scatter.15.cloned.1.call-done) | copy-start | bytes 196612
Sparse Core Ops, SparseCore 0:
  156.4 48.5 reduce-scatter.10
  208.7 61.9 reduce-scatter.18
  274.0 60.9 reduce-scatter.16
  338.6 60.9 reduce-scatter.14
  401.6 43.1 all-gather.1
  448.2 66.6 reduce-scatter.22
  518.4 66.7 reduce-scatter.20
  588.6 63.8 reduce-scatter.12
  656.3 62.3 reduce-scatter.24
